TPU v7x, 256 devices: a whole 4x4x8 slice. The times are simulated.
256 devices in a mesh: img: 32 (over z, y_hi, core), ori: 8 (over x, y_lo).
Axes of the slice: x: 4, y: 4 (y_hi: 2, y_lo: 2; y = y_hi * 2 + y_lo), z: 8, core: 2. Of those that a mesh axis runs over, the one named last changes fastest.
Arguments:
- images: float32 [32768, 2048], P(('img', 'ori')), may hold values from -40 to 40
- precision: float32 [32768], P('img'), may hold values from 0.5 to 2
- projections: bfloat16 [8192, 2048], P('ori'), may hold values from -1 to 1
- tile_mask: int32 [256, 64], P('img', 'ori'), may hold values from 0 to 1, as said below
Outputs:
- posteriors: bfloat16 [32768, 8192], P('img', 'ori')
- references: float32 [8192, 2048], P(('ori', 'img'))
Inputs may be any that keep to these rules, and one draw needn't show every extreme that they name: `tile_mask`: every image block has at least one live tile.
All inputs are finite; a program needn't handle non-finite values.
Results may differ from a plain program's by a relative error of at most 0.0095.
Values may be sent and summed in bfloat16 or wider, within the bound.
A program may use at most 64 MiB of HBM per device.

v0:
```python
import jax
import jax.numpy as jnp
from jax import lax
from jax.sharding import PartitionSpec as P

prior_weight = 1.0
very_low = -1e30


def weighted_sums(weights, rows_block):
    return lax.dot_general(
        weights, rows_block, (((0,), (0,)), ((), ())), preferred_element_type=jnp.float32
    )


def body(images, precision, projections, tile_mask):
    lowered = images.astype(jnp.bfloat16)
    grouped = lax.all_gather(lowered, "ori", axis=0, tiled=True)
    proj_float = projections.astype(jnp.float32)
    squared = jnp.sum(proj_float * proj_float, axis=1)
    blocks, tiles_here = tile_mask.shape
    per_block = grouped.shape[0] // blocks
    tile_width = projections.shape[0] // tiles_here
    products = lax.dot_general(
        grouped, projections, (((1,), (1,)), ((), ())), preferred_element_type=jnp.float32
    )
    scores = precision[:, None] * (products - 0.5 * squared[None, :])
    shaped = scores.reshape(blocks, per_block, tiles_here, tile_width)
    alive = jnp.broadcast_to((tile_mask > 0)[:, None, :, None], shaped.shape)
    masked = jnp.where(alive, shaped, very_low)
    local_high = jnp.max(masked, axis=(2, 3))
    row_high = lax.pmax(local_high, "ori")
    local_total = jnp.sum(
        jnp.where(alive, jnp.exp(masked - row_high[:, :, None, None]), 0.0), axis=(2, 3)
    )
    row_total = lax.psum(local_total, "ori")
    probable = (
        jnp.where(alive, jnp.exp(masked - row_high[:, :, None, None]), 0.0)
        / row_total[:, :, None, None]
    )
    posteriors = probable.reshape(scores.shape).astype(jnp.bfloat16)
    counts = jnp.sum(posteriors.astype(jnp.float32), axis=0)
    summed, totals = (
        lax.psum_scatter(
            weighted_sums(posteriors, grouped), "img", scatter_dimension=0, tiled=True
        ),
        lax.psum_scatter(counts, "img", scatter_dimension=0, tiled=True),
    )
    rows_here = summed.shape[0]
    first_row = lax.axis_index("img") * rows_here
    prior_rows = lax.dynamic_slice_in_dim(proj_float, first_row, rows_here, 0)
    refined = (summed + prior_weight * prior_rows) / (totals[:, None] + prior_weight)
    return (posteriors, refined)


def solution(mesh):
    return jax.shard_map(
        body,
        mesh=mesh,
        in_specs=(P(("img", "ori"), None), P("img"), P("ori", None), P("img", "ori")),
        out_specs=(P("img", "ori"), P(("ori", "img"), None)),
        check_vma=False,
    )
```

profile of v0, /device:TPU:2, one launch (start us, length us, event | category | flops | bytes accessed | tf_op | source)
XLA Modules:
  0.0 328.1 jit_solution(5797426212921994888)
XLA Ops:
  7.2 0.0 copy-start
  7.2 0.0 all-gather.2.cloned.1.call-start
  7.2 2.1 convert_element_type.12
  9.3 0.0 all-gather.2.cloned.1.call-update
  9.3 0.0 reduce-scatter.2.cloned.1.call-start
  9.4 0.7 broadcast_compare_fusion
  10.1 0.1 copy.8
  10.2 3.1 multiply_reduce_fusion
  13.2 92.3 %all-gather.2.cloned.1.call-done = bf16[1024,2048]{1,0:T(8,128)(2,1)} async-done(((bf16[128,2048]{1,0:T(8,128)(2,1)}), bf16[1024,2048]{1,0:T(8,128)(2,1)}) %all-gather.2.cloned.1.call-update) | async-done | bytes 4194320 | tf_op jit(solution)/shard_map/all_gather | solution.py:18
  105.5 0.3 broadcast_in_dim.22
  105.9 0.0 copy-done
  105.9 10.2 %fusion = (f32[1024]{0:T(1024)S(1)}, f32[1024,1024]{0,1:T(8,128)}) fusion(pred[128,8,8,128]{3,2,1,0:T(8,128)(4,1)S(1)} %bitcast.21, f32[1024]{0:T(1024)S(1)} %broadcast_multiply_fusion, f32[1024]{0:T(1024)S(1)} %copy-done, bf16[1024,2048]{1,0:T(8,128)(2,1)} %all-gather.2.cloned.1.call-done, bf16[1024,2048]{1,0:T(8,128)(2,1)} %param.6), kind=kOutput, calls=%fused_computation.5 | convolution fusion | flops 4299160576 | bytes 13643776 | tf_op jit(solution)/shard_map/dot_general | solution.py:24
  116.1 16.3 %pmax.7 = f32[1024]{0:T(1024)S(1)} all-reduce(f32[1024]{0:T(1024)S(1)} %get-tuple-element.8), channel_id=1, replica_groups=mesh['img'=32,'ori'=8] {'ori'}, use_global_device_ids=true, to_apply=%region_2.3 | all-reduce | flops 1024 | bytes 8192 | tf_op jit(solution)/shard_map/pmax | solution.py:32
  132.4 3.7 %fusion.1 = f32[1024]{0:T(1024)S(1)} fusion(f32[1024]{0:T(1024)S(1)} %pmax.7, f32[1024,1024]{0,1:T(8,128)} %get-tuple-element.9, f32[1024]{0:T(1024)S(1)} %broadcast_multiply_fusion, f32[1024]{0:T(1024)S(1)} %copy-done, pred[128,8,8,128]{3,2,1,0:T(8,128)(4,1)S(1)} %bitcast.22), kind=kLoop, calls=%fused_computation.6 | loop fusion | flops 6290432 | bytes 5259264 | tf_op jit(solution)/shard_map/reduce_sum | solution.py:33
  136.1 16.0 %psum.7 = f32[1024]{0:T(1024)S(1)} all-reduce(f32[1024]{0:T(1024)S(1)} %fusion.1), channel_id=1, replica_groups=mesh['img'=32,'ori'=8] {'ori'}, use_global_device_ids=true, to_apply=%region_4.5 | all-reduce | flops 1024 | bytes 8192 | tf_op jit(solution)/shard_map/psum | solution.py:36
  152.0 0.0 copy-start.1
  152.0 4.0 %convert_reduce_fusion = (f32[1024]{0:T(1024)S(1)}, bf16[1024,1024]{0,1:T(8,128)(2,1)S(1)}) fusion(f32[1024]{0:T(1024)S(1)} %psum.7, f32[1024]{0:T(1024)S(1)} %pmax.7, f32[1024,1024]{0,1:T(8,128)} %get-tuple-element.9, f32[1024]{0:T(1024)S(1)} %broadcast_multiply_fusion, f32[1024]{0:T(1024)S(1)} %copy-done, pred[128,8,8,128]{3,2,1,0:T(8,128)(4,1)S(1)} %bitcast.23), kind=kLoop, calls=%fused_computation.1 | loop fusion | flops 9436160 | bytes 7360512 | tf_op jit(solution)/shard_map/reduce_sum | solution.py:42
  156.0 0.0 copy-done.1
  156.0 6.6 %fusion.2 = f32[1024,2048]{1,0:T(8,128)} fusion(bf16[1024,1024]{0,1:T(8,128)(2,1)S(1)} %get-tuple-element.7, bf16[1024,2048]{1,0:T(8,128)(2,1)S(1)} %copy-done.1), kind=kOutput, calls=%fused_computation.11 | convolution fusion | flops 4294967296 | bytes 14680064 | tf_op jit(solution)/shard_map/dot_general | solution.py:11
  162.7 0.0 reduce-scatter.2.cloned.1.call-update
  162.7 0.0 copy-start.2
  162.7 6.5 %convert_element_type.13 = f32[1024,2048]{1,0:T(8,128)} convert(bf16[1024,2048]{1,0:T(8,128)(2,1)} %param.6) | non-fusion elementwise | flops 2097152 | bytes 12582912 | tf_op jit(solution)/shard_map/convert_element_type | solution.py:19
  169.2 0.0 copy-done.2
  169.2 0.6 dynamic-slice
  170.4 2.6 copy.9
  173.0 65.6 %all-reduce = f32[1024]{0:T(1024)S(1)} all-reduce(f32[1024]{0:T(1024)S(1)} %get-tuple-element.6), channel_id=3, replica_groups=mesh['img'=32,'ori'=8] {'img'}, use_global_device_ids=true, to_apply=%region_7.8.clone | all-reduce | flops 1024 | bytes 8192
  238.6 0.1 dynamic-slice_add_fusion
  238.6 80.8 %reduce-scatter.2.cloned.1.call-done = f32[32,2048]{1,0:T(8,128)} async-done(((f32[1024,2048]{1,0:T(8,128)}), f32[32,2048]{1,0:T(8,128)}) %reduce-scatter.2.cloned.1.call-update) | async-done | bytes 262160 | tf_op jit(solution)/shard_map/reduce_scatter | solution.py:44
  319.4 1.8 add_divide_fusion
  (1 shorter events, 0.0 us)
Async XLA Ops:
  7.2 98.7 %copy-start = (f32[1024]{0:T(1024)S(1)}, f32[1024]{0:T(1024)}, u32[]{:S(2)}) copy-start(f32[1024]{0:T(1024)} %param.5) | copy-start | bytes 12292
  7.2 98.4 %all-gather.2.cloned.1.call-start = ((), (), s32[]{:S(2)}) async-start(), calls=%async_computation.1 | async-start | bytes 4718592 | tf_op jit(solution)/shard_map/all_gather | solution.py:18
  9.3 310.1 %reduce-scatter.2.cloned.1.call-start = ((), (), s32[]{:S(2)}) async-start(), calls=%async_computation.2 | async-start | bytes 8650752 | tf_op jit(solution)/shard_map/reduce_scatter | solution.py:44
  152.0 4.0 %copy-start.1 = (bf16[1024,2048]{1,0:T(8,128)(2,1)S(1)}, bf16[1024,2048]{1,0:T(8,128)(2,1)}, u32[]{:S(2)}) copy-start(bf16[1024,2048]{1,0:T(8,128)(2,1)} %all-gather.2.cloned.1.call-done) | copy-start | bytes 12582916
  162.7 6.5 %copy-start.2 = (u32[256]{0:T(256)S(1)}, u32[256]{0:T(256)}, u32[]{:S(2)}) copy-start(u32[256]{0:T(256)} %constant.27) | copy-start | bytes 3076
Sparse Core Ops, SparseCore 0:
  10.3 95.1 all-gather.1
  162.8 156.5 reduce-scatter.1
where the time goes:
time: 328 us
  waiting for transfers between devices  173 us (53%)
  blocking collectives  97.8 us (30%)
  other arithmetic  21.9 us (7%)
  matrix products  16.8 us (5%)
  between operations  14.8 us (5%)
  local copies, waits for them, and re-layouts  3.58 us (1%)
    all_gather x1, waiting for transfers between devices, body(): grouped = lax.all_gather(lowered, 'ori', axis=0, tiled=True)  92.3 us
    reduce_scatter x1, waiting for transfers between devices, body(): lax.psum_scatter(weighted_sums(posteriors, grouped), 'img', scatter_dimen...  80.8 us
    unnamed x1, blocking collectives  65.6 us
    pmax x1, blocking collectives, body(): row_high = lax.pmax(local_high, 'ori')  16.3 us
    psum x1, blocking collectives, body(): row_total = lax.psum(local_total, 'ori')  16 us
    dot_general x1, matrix products, body(): lax.dot_general(grouped, projections, (((1,), (1,)), ((), ())), preferred...  10.2 us
    dot_general x1, matrix products, weighted_sums(): lax.dot_general(weights, rows_block, (((0,), (0,)), ((), ())), preferred_...  6.65 us
  transfers between devices with their start and end apart: 2, of which 2 were waited for; matrix products, arithmetic and copies ran while one was open for 4% of the time, Pallas kernels for 0%

commit v1 on v0

--- a/solution.py
+++ b/solution.py
@@ -15,7 +15,10 @@
 
 def body(images, precision, projections, tile_mask):
     lowered = images.astype(jnp.bfloat16)
-    grouped = lax.all_gather(lowered, "ori", axis=0, tiled=True)
+    size = lax.axis_size("ori")
+    pieces = jnp.stack([lowered for _ in range(size)])
+    pieces = lax.all_to_all(pieces, "ori", split_axis=0, concat_axis=0)
+    grouped = jnp.concatenate(pieces, axis=0)
     proj_float = projections.astype(jnp.float32)
     squared = jnp.sum(proj_float * proj_float, axis=1)
     blocks, tiles_here = tile_mask.shape

time: 328 us -> 302 us (0.921)
  waiting for transfers between devices: 173 us -> 132 us
  starting transfers between devices: 0.08 us -> 6.86 us
  blocking collectives: 97.8 us -> 103 us
    all_gather x1 -> x0, waiting for transfers between devices: 92.3 us -> none  [body(): grouped = lax.all_gather(lowered, 'ori', axis=0, tiled=True)]
    all_to_all x0 -> x1, waiting for transfers between devices: none -> 52.1 us  [body(): pieces = lax.all_to_all(pieces, 'ori', split_axis=0, concat_axis=0)]
    all_to_all x0 -> x1, starting transfers between devices: none -> 6.85 us  [body(): pieces = lax.all_to_all(pieces, 'ori', split_axis=0, concat_axis=0)]
where the time goes in v1:
time: 302 us; the launch traced here: 301 us
  waiting for transfers between devices  132 us (44%)
  blocking collectives  103 us (34%)
  other arithmetic  20.3 us (7%)
  matrix products  19 us (6%)
  between operations  14.8 us (5%)
  starting transfers between devices  6.86 us (2%)
  local copies, waits for them, and re-layouts  6.04 us (2%)
    reduce_scatter x1, waiting for transfers between devices, body(): lax.psum_scatter(weighted_sums(posteriors, grouped), 'img', scatter_dimen...  79.8 us
    unnamed x1, blocking collectives  67.9 us
    all_to_all x1, waiting for transfers between devices, body(): pieces = lax.all_to_all(pieces, 'ori', split_axis=0, concat_axis=0)  52.1 us
    pmax x1, blocking collectives, body(): row_high = lax.pmax(local_high, 'ori')  17.4 us
    psum x1, blocking collectives, body(): row_total = lax.psum(local_total, 'ori')  17.2 us
    dot_general x1, matrix products, body(): lax.dot_general(grouped, projections, (((1,), (1,)), ((), ())), preferred...  10.1 us
    dot_general x1, matrix products, weighted_sums(): lax.dot_general(weights, rows_block, (((0,), (0,)), ((), ())), preferred_...  8.86 us
    all_to_all x1, starting transfers between devices, body(): pieces = lax.all_to_all(pieces, 'ori', split_axis=0, concat_axis=0)  6.85 us
  transfers between devices with their start and end apart: 2, of which 2 were waited for; matrix products, arithmetic and copies ran while one was open for 4% of the time, Pallas kernels for 0%

profile of v1, /device:TPU:2, one launch (start us, length us, event | category | flops | bytes accessed | tf_op | source)
XLA Modules:
  0.0 301.4 jit_solution(15294209598058272453)
XLA Ops:
  7.2 1.3 convert_element_type.12
  8.5 2.5 stack.2
  10.9 0.0 copy-start.1
  10.9 6.9 %all-to-all-start = ((bf16[8,128,2048]{2,1,0:T(8,128)(2,1)}), bf16[8,128,2048]{2,1,0:T(8,128)(2,1)}, u32[]{:S(2)}, u32[]{:S(2)}) async-start(bf16[8,128,2048]{2,1,0:T(8,128)(2,1)} %stack.2), calls=%async_computation | async-start | bytes 8388608 | tf_op jit(solution)/shard_map/all_to_all | solution.py:20
  17.8 0.0 copy-start
  17.8 0.0 reduce-scatter.2.cloned.1.call-start
  17.8 0.0 copy-done.1
  17.8 0.1 copy.8
  17.9 3.1 %multiply_reduce_fusion = f32[1024]{0:T(1024)S(1)} fusion(bf16[1024,2048]{1,0:T(8,128)(2,1)} %param.6), kind=kLoop, calls=%fused_computation | loop fusion | flops 6290432 | bytes 4198400 | tf_op jit(solution)/shard_map/reduce_sum | solution.py:23
  21.0 52.1 %all-to-all-done = bf16[8,128,2048]{2,1,0:T(8,128)(2,1)} async-done(((bf16[8,128,2048]{2,1,0:T(8,128)(2,1)}), bf16[8,128,2048]{2,1,0:T(8,128)(2,1)}, u32[]{:S(2)}, u32[]{:S(2)}) %all-to-all-start) | async-done | bytes 4194336 | tf_op jit(solution)/shard_map/all_to_all | solution.py:20
  73.1 0.3 broadcast_in_dim.22
  73.4 0.0 copy-done
  73.4 10.1 %fusion = (f32[1024]{0:T(1024)S(1)}, f32[1024,1024]{0,1:T(8,128)}) fusion(pred[128,8,8,128]{3,2,1,0:T(8,128)(4,1)S(1)} %bitcast.22, f32[1024]{0:T(1024)S(1)} %broadcast_multiply_fusion, f32[1024]{0:T(1024)S(1)} %copy-done, bf16[1024,2048]{1,0:T(8,128)(2,1)} %bitcast, bf16[1024,2048]{1,0:T(8,128)(2,1)} %param.6), kind=kOutput, calls=%fused_computation.5 | convolution fusion | flops 4299160576 | bytes 13643776 | tf_op jit(solution)/shard_map/dot_general | solution.py:27
  83.6 17.4 %pmax.7 = f32[1024]{0:T(1024)S(1)} all-reduce(f32[1024]{0:T(1024)S(1)} %get-tuple-element.8), channel_id=1, replica_groups=mesh['img'=32,'ori'=8] {'ori'}, use_global_device_ids=true, to_apply=%region_2.3 | all-reduce | flops 1024 | bytes 8192 | tf_op jit(solution)/shard_map/pmax | solution.py:35
  101.0 3.7 %fusion.1 = f32[1024]{0:T(1024)S(1)} fusion(f32[1024]{0:T(1024)S(1)} %pmax.7, f32[1024,1024]{0,1:T(8,128)} %get-tuple-element.9, f32[1024]{0:T(1024)S(1)} %broadcast_multiply_fusion, f32[1024]{0:T(1024)S(1)} %copy-done, pred[128,8,8,128]{3,2,1,0:T(8,128)(4,1)S(1)} %bitcast.23), kind=kLoop, calls=%fused_computation.6 | loop fusion | flops 6290432 | bytes 5259264 | tf_op jit(solution)/shard_map/reduce_sum | solution.py:36
  104.7 17.2 %psum.7 = f32[1024]{0:T(1024)S(1)} all-reduce(f32[1024]{0:T(1024)S(1)} %fusion.1), channel_id=1, replica_groups=mesh['img'=32,'ori'=8] {'ori'}, use_global_device_ids=true, to_apply=%region_4.5 | all-reduce | flops 1024 | bytes 8192 | tf_op jit(solution)/shard_map/psum | solution.py:39
  121.9 3.8 %convert_reduce_fusion = (f32[1024]{0:T(1024)S(1)}, bf16[1024,1024]{0,1:T(8,128)(2,1)S(1)}) fusion(f32[1024]{0:T(1024)S(1)} %psum.7, f32[1024]{0:T(1024)S(1)} %pmax.7, f32[1024,1024]{0,1:T(8,128)} %get-tuple-element.9, f32[1024]{0:T(1024)S(1)} %broadcast_multiply_fusion, f32[1024]{0:T(1024)S(1)} %copy-done, pred[128,8,8,128]{3,2,1,0:T(8,128)(4,1)S(1)} %bitcast.24), kind=kLoop, calls=%fused_computation.1 | loop fusion | flops 9436160 | bytes 7360512 | tf_op jit(solution)/shard_map/reduce_sum | solution.py:45
  125.7 8.9 %fusion.2 = f32[1024,2048]{1,0:T(8,128)} fusion(bf16[1024,1024]{0,1:T(8,128)(2,1)S(1)} %get-tuple-element.7, bf16[1024,2048]{1,0:T(8,128)(2,1)} %bitcast), kind=kOutput, calls=%fused_computation.11 | convolution fusion | flops 4294967296 | bytes 14680064 | tf_op jit(solution)/shard_map/dot_general | solution.py:11
  134.6 0.0 reduce-scatter.2.cloned.1.call-update
  134.6 0.0 copy-start.2
  134.7 6.5 %convert_element_type.13 = f32[1024,2048]{1,0:T(8,128)} convert(bf16[1024,2048]{1,0:T(8,128)(2,1)} %param.6) | non-fusion elementwise | flops 2097152 | bytes 12582912 | tf_op jit(solution)/shard_map/convert_element_type | solution.py:22
  141.1 0.0 copy-done.2
  141.1 0.6 dynamic-slice
  142.4 2.6 copy.9
  144.9 67.9 %all-reduce = f32[1024]{0:T(1024)S(1)} all-reduce(f32[1024]{0:T(1024)S(1)} %get-tuple-element.6), channel_id=3, replica_groups=mesh['img'=32,'ori'=8] {'img'}, use_global_device_ids=true, to_apply=%region_7.8.clone | all-reduce | flops 1024 | bytes 8192
  212.9 0.1 dynamic-slice_add_fusion
  212.9 79.8 %reduce-scatter.2.cloned.1.call-done = f32[32,2048]{1,0:T(8,128)} async-done(((f32[1024,2048]{1,0:T(8,128)}), f32[32,2048]{1,0:T(8,128)}) %reduce-scatter.2.cloned.1.call-update) | async-done | bytes 262160 | tf_op jit(solution)/shard_map/reduce_scatter | solution.py:47
  292.7 1.8 add_divide_fusion
  (2 shorter events, 0.0 us)
Async XLA Ops:
  10.9 6.9 %copy-start.1 = (s32[8,8]{1,0:T(8,128)S(1)}, s32[8,8]{1,0:T(8,128)}, u32[]{:S(2)}) copy-start(s32[8,8]{1,0:T(8,128)} %param.7) | copy-start | bytes 772
  10.9 62.2 %all-to-all-start = ((bf16[8,128,2048]{2,1,0:T(8,128)(2,1)}), bf16[8,128,2048]{2,1,0:T(8,128)(2,1)}, u32[]{:S(2)}, u32[]{:S(2)}) async-start(bf16[8,128,2048]{2,1,0:T(8,128)(2,1)} %stack.2), calls=%async_computation | async-start | bytes 8388608 | tf_op jit(solution)/shard_map/all_to_all | solution.py:20
  17.8 55.7 %copy-start = (f32[1024]{0:T(1024)S(1)}, f32[1024]{0:T(1024)}, u32[]{:S(2)}) copy-start(f32[1024]{0:T(1024)} %param.5) | copy-start | bytes 12292
  17.8 274.9 %reduce-scatter.2.cloned.1.call-start = ((), (), s32[]{:S(2)}) async-start(), calls=%async_computation.2 | async-start | bytes 8650752 | tf_op jit(solution)/shard_map/reduce_scatter | solution.py:47
  134.6 6.5 %copy-start.2 = (u32[256]{0:T(256)S(1)}, u32[256]{0:T(256)}, u32[]{:S(2)}) copy-start(u32[256]{0:T(256)} %constant.27) | copy-start | bytes 3076
Sparse Core Ops, SparseCore 0:
  134.8 157.8 reduce-scatter.1
